TPU v7x, 256 devices: a whole 4x4x8 slice. The times are simulated.
256 devices in a mesh: fact: 64 (over z, y, core), feat: 4 (over x).
Axes of the slice: x: 4, y: 4, z: 8, core: 2. Of those that a mesh axis runs over, the one named last changes fastest.
Arguments:
- fact_x: bfloat16 [65536, 512], P('fact', 'feat'), may hold values from -16 to 16
- dim_owner: int32 [65536, 1], P('fact'), may hold values from 0 to 63; in each aligned block of 1024 rows (0 to 1023, 1024 to 2047, ...) at most 48 rows name the same one
- dim_slot: int32 [65536], P('fact'), may hold values from 0 to 127
- fact_owner: int32 [65536, 1], P('fact'), may hold values from 0 to 63; in each aligned block of 1024 rows (0 to 1023, 1024 to 2047, ...) at most 48 rows name the same one
- fact_slot: int32 [65536], P('fact'), may hold values from 0 to 127
- dim_table: bfloat16 [8192, 512], P('fact', 'feat'), may hold values from -6 to 6
- entity_h: bfloat16 [8192, 512], P('fact', 'feat'), may hold values from -16 to 16
- w_msg: bfloat16 [512, 512], P(None, 'feat'), may hold values from -0.25 to 0.25
- w_self: bfloat16 [512, 512], P(None, 'feat'), may hold values from -0.25 to 0.25
- w_neigh: bfloat16 [512, 512], P(None, 'feat'), may hold values from -0.25 to 0.25
- cotangent: bfloat16 [8192, 512], P('fact', 'feat'), may hold values from -0.59765625 to 0.59765625
Outputs:
- output_h: bfloat16 [8192, 512], P('fact', 'feat')
- grad_w_msg: float32 [512, 512], P('fact', 'feat')
- grad_w_self: float32 [512, 512], P('fact', 'feat')
- grad_w_neigh: float32 [512, 512], P('fact', 'feat')
- grad_dim: float32 [8192, 512], P('fact', 'feat')
Inputs may be any that keep to these rules, and one draw needn't show every extreme that they name: `fact_owner`: among the fact rows of one index of fact, no key range is named by more than 48 rows, and some key range by exactly 48. `dim_owner`: among the fact rows of one index of fact, no block of the dimension table is named by more than 48 rows, and some block by exactly 48.
All inputs are finite; a program needn't handle non-finite values.
Results may differ from a plain program's by a relative error of at most 0.0059.
Values may be sent and summed in bfloat16 or wider, within the bound.
A program may use at most 64 MiB of HBM per device.

v0:
```python
import math

import jax
import jax.numpy as jnp
from jax import lax
from jax.sharding import PartitionSpec as P


def silu_slope(values):
    sigmoid_v = jax.nn.sigmoid(values)
    return sigmoid_v * (1.0 + values * (1.0 - sigmoid_v))


def pick_rows(row_keys, table):
    table_rows = table.shape[0]
    block_len = math.gcd(table_rows, 1024)
    num_blocks = table_rows // block_len
    blocks = table.reshape(num_blocks, block_len, table.shape[1])
    columns = lax.iota(jnp.int32, block_len)

    def advance(running, block_no):
        block = lax.dynamic_index_in_dim(blocks, block_no, 0, keepdims=False)
        selector = (row_keys[:, None] == block_no * block_len + columns[None, :]).astype(
            jnp.bfloat16
        )
        return (running + jnp.dot(selector, block, preferred_element_type=jnp.float32), None)

    initial = jnp.zeros((row_keys.shape[0], table.shape[1]), jnp.float32)
    running, _ = lax.scan(advance, initial, jnp.arange(num_blocks, dtype=jnp.int32))
    return running


def sum_rows(row_keys, values, extent):
    block_len = math.gcd(extent, 1024)
    num_blocks = extent // block_len
    targets = lax.iota(jnp.int32, block_len)

    def column_block(block_no):
        selector = (row_keys[None, :] - block_no * block_len == targets[:, None]).astype(
            jnp.bfloat16
        )
        return jnp.dot(selector, values, preferred_element_type=jnp.float32)

    stacked = lax.map(column_block, jnp.arange(num_blocks, dtype=jnp.int32))
    return stacked.reshape(extent, values.shape[1])


def shards(
    fact_x,
    dim_owner,
    dim_slot,
    fact_owner,
    fact_slot,
    dim_table,
    entity_h,
    w_msg,
    w_self,
    w_neigh,
    cotangent,
):
    ent_rows = entity_h.shape[0]
    dim_local = dim_table.shape[0]
    owners = lax.axis_size("fact")
    owner_ids = fact_owner[:, 0]
    entity = owner_ids * ent_rows + fact_slot
    dim_blocks = dim_owner[:, 0]
    fact_dim = dim_blocks * dim_local + dim_slot
    x_full = lax.all_gather(fact_x, "feat", axis=1, tiled=True)
    looked = pick_rows(fact_dim, lax.all_gather(dim_table, "fact", axis=0, tiled=True))
    msg_pre = jnp.dot(x_full, w_msg, preferred_element_type=jnp.float32) + looked
    message = jax.nn.silu(msg_pre).astype(jnp.bfloat16)
    entity_sums = lax.psum_scatter(
        sum_rows(entity, message, ent_rows * lax.axis_size("fact")),
        "fact",
        scatter_dimension=0,
        tiled=True,
    )
    hits = jnp.zeros((ent_rows * owners,), jnp.float32).at[entity].add(1.0)
    counts = lax.psum_scatter(hits, "fact", scatter_dimension=0, tiled=True)
    divisor = jnp.maximum(counts, 1.0)
    aggregate = (entity_sums / divisor[:, None]).astype(jnp.bfloat16)
    h_full, agg_full = (
        lax.all_gather(entity_h, "feat", axis=1, tiled=True),
        lax.all_gather(aggregate, "feat", axis=1, tiled=True),
    )
    pre_act = jnp.dot(h_full, w_self, preferred_element_type=jnp.float32) + jnp.dot(
        agg_full, w_neigh, preferred_element_type=jnp.float32
    )
    output_h = jax.nn.silu(pre_act).astype(jnp.bfloat16)
    d_pre = (cotangent.astype(jnp.float32) * silu_slope(pre_act)).astype(jnp.bfloat16)
    agg_term = jnp.einsum("ej,aj->ea", d_pre, w_neigh, preferred_element_type=jnp.float32)
    d_agg = lax.psum_scatter(agg_term, "feat", scatter_dimension=1, tiled=True)
    d_scaled = (d_agg / divisor[:, None]).astype(jnp.bfloat16)
    d_message = pick_rows(entity, lax.all_gather(d_scaled, "fact", axis=0, tiled=True)).astype(
        jnp.bfloat16
    )
    d_msgpre = (d_message.astype(jnp.float32) * silu_slope(msg_pre)).astype(jnp.bfloat16)
    grad_dim = lax.psum_scatter(
        sum_rows(fact_dim, d_msgpre, dim_local * lax.axis_size("fact")),
        "fact",
        scatter_dimension=0,
        tiled=True,
    )
    self_part = jnp.einsum("ea,eb->ab", h_full, d_pre, preferred_element_type=jnp.float32)
    neigh_part = jnp.einsum("ea,eb->ab", agg_full, d_pre, preferred_element_type=jnp.float32)
    msg_part = jnp.einsum("fa,fb->ab", x_full, d_msgpre, preferred_element_type=jnp.float32)
    grad_w_self, grad_w_neigh, grad_w_msg = (
        lax.psum_scatter(self_part, "fact", scatter_dimension=0, tiled=True),
        lax.psum_scatter(neigh_part, "fact", scatter_dimension=0, tiled=True),
        lax.psum_scatter(msg_part, "fact", scatter_dimension=0, tiled=True),
    )
    return (output_h, grad_w_msg, grad_w_self, grad_w_neigh, grad_dim)


def solution(mesh):
    placed = (
        P("fact", "feat"),
        P("fact", None),
        P("fact"),
        P("fact", None),
        P("fact"),
        P("fact", "feat"),
        P("fact", "feat"),
        P(None, "feat"),
        P(None, "feat"),
        P(None, "feat"),
        P("fact", "feat"),
    )
    return jax.shard_map(
        shards,
        mesh=mesh,
        in_specs=placed,
        out_specs=(
            P("fact", "feat"),
            P("fact", "feat"),
            P("fact", "feat"),
            P("fact", "feat"),
            P("fact", "feat"),
        ),
        check_vma=False,
    )
```

profile of v0, /device:TPU:8, one launch (start us, length us, event | category | flops | bytes accessed | tf_op | source)
XLA Modules:
  0.0 918.6 jit_solution(5410309900059285577)
XLA Ops:
  11.5 78.5 %all-gather.6.cloned.1.call-done = bf16[8192,128]{1,0:T(8,128)(2,1)} async-done(((bf16[128,128]{1,0:T(8,128)(2,1)}), bf16[8192,128]{1,0:T(8,128)(2,1)}) %all-gather.6.cloned.1.call-update) | async-done | bytes 2097168 | tf_op jit(solution)/shard_map/all_gather | solution.py:69
  90.0 40.7 %while.46 = (s32[]{:T(128)}, f32[1024,128]{1,0:T(8,128)S(1)}, s32[1024]{0:T(1024)S(1)}, s32[8]{0:T(128)S(1)}, bf16[8,1024,128]{2,1,0:T(8,128)(2,1)}, /*index=5*/s32[]{:T(128)}, s32[]{:T(128)}, s32[]{:T(128)}, s32[]{:T(128)}) while((s32[]{:T(128)}, f32[1024,128]{1,0:T(8,128)S(1)}, s32[1024]{0:T(1024)S(1)}, s32[8]{0:T(128)S(1)}, ...), condition=%wide.region_1.2_spmd.clone, body=%wide.region_0.1_spmd.clone.sunk | while | flops 269747200 | bytes 1323177 | solution.py:29
  93.2 1.9 fusion.73
  98.3 1.9 fusion.73
  103.4 1.9 fusion.73
  108.5 1.9 fusion.73
  113.6 1.9 fusion.73
  118.6 1.9 fusion.73
  123.7 1.9 fusion.73
  128.8 1.9 fusion.73
  130.7 1.7 multiply_convert_fusion.1
  132.4 2.3 broadcast.43.clone
  134.7 22.6 %while.44 = (s32[]{:T(128)}, f32[8,1024,128]{2,1,0:T(8,128)}, s32[8]{0:T(128)S(1)}, s32[1024]{0:T(1024)S(1)}, bf16[1024,128]{1,0:T(8,128)(2,1)S(1)}, /*index=5*/s32[]{:T(128)}, s32[1]{0:T(128)}) while((s32[]{:T(128)}, f32[8,1024,128]{2,1,0:T(8,128)}, s32[8]{0:T(128)S(1)}, s32[1024]{0:T(1024)S(1)}, bf16[1024,128]{1,0:T(8,128)(2,1)S(1)}, ...), condition=%wide.region_3.4_spmd.clone, body=%wide.region_2.3_spmd.clone.sunk | while | flops 269485056 | bytes 799337 | solution.py:44
  159.3 5.9 scatter_custom_fusion
  165.2 244.8 %all-reduce = f32[8192]{0:T(1024)S(1)} all-reduce(f32[8192]{0:T(1024)S(1)} %scatter_custom_fusion), channel_id=3, replica_groups=mesh['fact'=64,'feat'=4] {'fact'}, use_global_device_ids=true, to_apply=%region_6.7.clone | all-reduce | flops 8192 | bytes 65536
  410.1 11.5 %all_gather.15 = bf16[128,512]{1,0:T(8,128)(2,1)S(1)} all-gather(bf16[128,128]{1,0:T(8,128)(2,1)S(1)} %copy-done.4), channel_id=1, replica_groups=mesh['fact'=64,'feat'=4] {'feat'}, dimensions={1}, use_global_device_ids=true | all-gather | bytes 163840 | tf_op jit(solution)/shard_map/all_gather | solution.py:83
  422.8 10.7 %all_gather.18 = bf16[128,512]{1,0:T(8,128)(2,1)S(1)} all-gather(bf16[128,128]{1,0:T(8,128)(2,1)S(1)} %divide_convert_fusion.1), channel_id=1, replica_groups=mesh['fact'=64,'feat'=4] {'feat'}, dimensions={1}, use_global_device_ids=true | all-gather | bytes 163840 | tf_op jit(solution)/shard_map/all_gather | solution.py:84
  435.3 25.3 %reduce-scatter.8.cloned.1.call-done = f32[128,128]{1,0:T(8,128)} async-done(((f32[128,512]{1,0:T(8,128)}), f32[128,128]{1,0:T(8,128)}) %reduce-scatter.8.cloned.1.call-update) | async-done | bytes 65552 | tf_op jit(solution)/shard_map/reduce_scatter | solution.py:92
  464.0 75.8 %all-gather.8.cloned.1.call-done = bf16[8192,128]{1,0:T(8,128)(2,1)} async-done(((bf16[128,128]{1,0:T(8,128)(2,1)}), bf16[8192,128]{1,0:T(8,128)(2,1)}) %all-gather.8.cloned.1.call-update) | async-done | bytes 2097168 | tf_op jit(solution)/shard_map/all_gather | solution.py:94
  539.8 40.7 %while.47 = (s32[]{:T(128)}, f32[1024,128]{1,0:T(8,128)S(1)}, s32[1024]{0:T(1024)S(1)}, s32[8]{0:T(128)S(1)}, bf16[8,1024,128]{2,1,0:T(8,128)(2,1)}, /*index=5*/s32[]{:T(128)}, s32[]{:T(128)}, s32[]{:T(128)}, s32[]{:T(128)}) while((s32[]{:T(128)}, f32[1024,128]{1,0:T(8,128)S(1)}, s32[1024]{0:T(1024)S(1)}, s32[8]{0:T(128)S(1)}, ...), condition=%wide.region_9.10_spmd.clone, body=%wide.region_8.9_spmd.clone.sunk | while | flops 269747200 | bytes 1323177 | solution.py:29
  543.0 1.9 fusion.76
  548.1 1.9 fusion.76
  553.2 1.9 fusion.76
  558.3 1.9 fusion.76
  563.4 1.9 fusion.76
  568.5 1.9 fusion.76
  573.6 1.9 fusion.76
  578.7 1.9 fusion.76
  581.9 2.3 broadcast.43
  584.2 22.6 %while.45 = (s32[]{:T(128)}, f32[8,1024,128]{2,1,0:T(8,128)}, s32[8]{0:T(128)S(1)}, s32[1024]{0:T(1024)S(1)}, bf16[1024,128]{1,0:T(8,128)(2,1)S(1)}, /*index=5*/s32[]{:T(128)}, s32[1]{0:T(128)}) while((s32[]{:T(128)}, f32[8,1024,128]{2,1,0:T(8,128)}, s32[8]{0:T(128)S(1)}, s32[1024]{0:T(1024)S(1)}, ...), condition=%wide.region_14.15_spmd.clone, body=%wide.region_13.14_spmd.clone.sunk | while | flops 269485056 | bytes 799337 | solution.py:44
  607.5 156.9 %all-reduce.7.cloned.1.call-done = (f32[512,128]{0,1:T(8,128)}, f32[512,128]{0,1:T(8,128)}, f32[512,128]{1,0:T(8,128)}) async-done(((f32[512,128]{0,1:T(8,128)}, f32[512,128]{0,1:T(8,128)}, f32[512,128]{1,0:T(8,128)}), (f32[512,128]{0,1:T(8,128)}, f32[512,128]{0,1:T(8,128)}, f32[512,128]{1,0:T(8,128)})) %all-reduce.7.cloned.1.call-update) | async-done | bytes 786448
  767.9 143.8 %reduce-scatter.10.cloned.1.call-done = f32[128,128]{1,0:T(8,128)} async-done(((f32[8192,128]{1,0:T(8,128)}), f32[128,128]{1,0:T(8,128)}) %reduce-scatter.10.cloned.1.call-update) | async-done | bytes 65552 | tf_op jit(solution)/shard_map/reduce_scatter | solution.py:98
  (136 shorter events, 60.9 us)
Async XLA Ops:
  7.2 123.6 %copy-start = (bf16[512,128]{1,0:T(8,128)(2,1)S(1)}, bf16[512,128]{1,0:T(8,128)(2,1)}, u32[]{:S(2)}) copy-start(bf16[512,128]{1,0:T(8,128)(2,1)} %param.26) | copy-start | bytes 393220
  7.2 82.8 %all-gather.6.cloned.1.call-start = ((), (), s32[]{:S(2)}) async-start(), calls=%async_computation.4 | async-start | bytes 2129920 | tf_op jit(solution)/shard_map/all_gather | solution.py:69
  7.9 122.8 %all-gather.4.cloned.1.call-start = ((), (), s32[]{:S(2)}) async-start(), calls=%async_computation.3 | async-start | bytes 1310720 | tf_op jit(solution)/shard_map/all_gather | solution.py:68
  8.7 413.2 %reduce-scatter.6.cloned.1.call-start = ((), (), s32[]{:S(2)}) async-start(), calls=%async_computation.5 | async-start | bytes 4259840 | tf_op jit(solution)/shard_map/reduce_scatter | solution.py:72
  157.4 0.7 copy-start.6
  157.4 252.7 %copy-start.4 = (bf16[128,128]{1,0:T(8,128)(2,1)S(1)}, bf16[128,128]{1,0:T(8,128)(2,1)}, u32[]{:S(2)}) copy-start(bf16[128,128]{1,0:T(8,128)(2,1)} %param.25) | copy-start | bytes 98308
  157.4 264.3 %copy-start.2 = (bf16[512,128]{1,0:T(8,128)(2,1)S(1)}, bf16[512,128]{1,0:T(8,128)(2,1)}, u32[]{:S(2)}) copy-start(bf16[512,128]{1,0:T(8,128)(2,1)} %param.27) | copy-start | bytes 393220
  157.4 276.1 %copy-start.3 = (bf16[512,128]{1,0:T(8,128)(2,1)S(1)}, bf16[512,128]{1,0:T(8,128)(2,1)}, u32[]{:S(2)}) copy-start(bf16[512,128]{1,0:T(8,128)(2,1)} %param.28) | copy-start | bytes 393220
  157.4 276.1 %copy-start.5 = (bf16[128,128]{1,0:T(8,128)(2,1)S(1)}, bf16[128,128]{1,0:T(8,128)(2,1)}, u32[]{:S(2)}) copy-start(bf16[128,128]{1,0:T(8,128)(2,1)} %param.29) | copy-start | bytes 98308
  157.4 303.1 %reduce-scatter.8.cloned.1.call-start = ((), (), s32[]{:S(2)}) async-start(), calls=%async_computation.6 | async-start | bytes 327680 | tf_op jit(solution)/shard_map/reduce_scatter | solution.py:92
  435.2 104.6 %all-gather.8.cloned.1.call-start = ((), (), s32[]{:S(2)}) async-start(), calls=%async_computation.7 | async-start | bytes 2129920 | tf_op jit(solution)/shard_map/all_gather | solution.py:94
  462.1 302.2 %all-reduce.7.cloned.1.call-start = ((), (), s32[]{:S(2)}) async-start(), calls=%async_computation.9 | async-start | bytes 1572864
  539.8 40.9 %copy-start.1 = (bf16[1024,512]{1,0:T(8,128)(2,1)S(1)}, bf16[1024,512]{1,0:T(8,128)(2,1)}, u32[]{:S(2)}) copy-start(bf16[1024,512]{1,0:T(8,128)(2,1)} %all-gather.4.cloned.1.call-done) | copy-start | bytes 3145732
  581.8 329.9 %reduce-scatter.10.cloned.1.call-start = ((), (), s32[]{:S(2)}) async-start(), calls=%async_computation.8 | async-start | bytes 4259840 | tf_op jit(solution)/shard_map/reduce_scatter | solution.py:98
Sparse Core Ops, SparseCore 0:
  10.8 79.1 all-gather.5
  91.8 27.0 all-gather.3
  157.5 141.6 reduce-scatter.5
  435.3 25.1 reduce-scatter.7
  463.8 76.0 all-gather.7
  582.0 182.3 all-reduce.6
  769.6 142.0 reduce-scatter.9
where the time goes:
time: 921 us; the launch traced here: 919 us
  waiting for transfers between devices  482 us (52%)
  blocking collectives  267 us (29%)
  matrix products  61.8 us (7%)
  loops' own time  52.5 us (6%)
  local copies, waits for them, and re-layouts  28 us (3%)
  between operations  15.6 us (2%)
  other arithmetic  11.6 us (1%)
    unnamed x1, blocking collectives  245 us
    unnamed x8, waiting for transfers between devices  158 us
    reduce_scatter x1, waiting for transfers between devices, shards(): lax.psum_scatter(sum_rows(fact_dim, d_msgpre, dim_local * lax.axis_size('...  144 us
    all_gather x1, waiting for transfers between devices, shards(): lax.all_gather(dim_table, 'fact', axis=0, tiled=True)  78.5 us
    all_gather x1, waiting for transfers between devices, shards(): lax.all_gather(d_scaled, 'fact', axis=0, tiled=True)  75.8 us
    another operation x2, loops' own time, pick_rows(): lax.scan(advance, initial, jnp.arange(num_blocks, dtype=jnp.int32))  42 us
    dot_general x16, matrix products, advance(): jnp.dot(selector, block, preferred_element_type=jnp.float32)  30 us
    dot_general x16, matrix products, column_block(): return jnp.dot(selector, values, preferred_element_type=jnp.float32)  25.3 us
  transfers between devices with their start and end apart: 7, of which 5 were waited for; matrix products, arithmetic and copies ran while one was open for 6% of the time, Pallas kernels for 0%

commit v1 on v0

v1 whole, which is shorter than its diff:
```python
import functools

import jax
import jax.numpy as jnp
from jax import lax
from jax.experimental import pallas as pl
from jax.experimental.pallas import tpu as pltpu
from jax.sharding import PartitionSpec as P

MESH = pl.DeviceIdType.MESH
BF = jnp.bfloat16
F32 = jnp.float32

NZ, NY = 8, 4
GATHER = (0, -1, 1, -2, 2, -3, 3, -4)
REDUCE = (4, -3, 3, -2, 2, -1, 1, 0)
YD = (1, 3, 2)
ROWS = 1024
TILE = 256
W = 128
EXTRA = 160


def sigmoid_of(v):
    return 1.0 / (1.0 + jnp.exp(-v))


def kernel(
    x_ref,
    dim_own_ref,
    dim_slot_ref,
    ent_own_ref,
    ent_slot_ref,
    table_ref,
    h_ref,
    w_msg_ref,
    w_self_ref,
    w_neigh_ref,
    cot_ref,
    out_ref,
    gwm_ref,
    gws_ref,
    gwn_ref,
    gdim_ref,
    xs,
    tab,
    b_dim,
    b_ent,
    bt_dim,
    bt_ent,
    o_dim,
    o_ent,
    ot_dim,
    ot_ent,
    acc,
    dmsg,
    slope,
    val,
    ch,
    cs,
    cr1,
    cr2,
    hx,
    cx,
    ax,
    w2,
    pre,
    gw,
    pown,
    yown,
    psend1,
    precv1,
    ysend1,
    yrecv1,
    zsend1,
    zrecv1,
    psend2,
    precv2,
    ysend2,
    yrecv2,
    zsend2,
    zrecv2,
    res1,
    res2,
    div,
    s_ch,
    r_ch,
    s_y,
    r_y,
    s_p,
    r_p,
    s_ch2,
    r_ch2,
    s_y2,
    r_y2,
    s_p2,
    r_p2,
    s_x,
    r_x,
    s_h,
    r_h,
    s_c,
    r_c,
    s_w,
    r_w,
    s_wp,
    r_wp,
    s_a,
    r_a,
    s_n1,
    r_n1,
    s_n2,
    r_n2,
):
    f = lax.axis_index("fact")
    g = lax.axis_index("feat")
    z, y, c = f // 8, lax.rem(f // 2, 4), lax.rem(f, 2)
    q = lax.rem(f, 8)

    def at(zz, yy, cc):
        return (zz * 4 + yy) * 2 + cc

    zs = [lax.rem(z + d, NZ) for d in range(NZ)]
    ys = [lax.rem(y + d, NY) for d in range(NY)]
    gs = [lax.rem(g + d, 4) for d in range(4)]
    right, left, mate = at(zs[1], y, c), at(zs[7], y, c), at(z, y, 1 - c)
    zpeer = [at(zs[d], y, c) for d in range(NZ)]
    ypeer = [at(z, ys[d], c) for d in YD]
    qpeer = [z * 8 + lax.rem(q + d, 8) for d in range(8)]

    def remote(src, dst, ssem, rsem, to_f, to_g=None):
        return pltpu.make_async_remote_copy(
            src_ref=src,
            dst_ref=dst,
            send_sem=ssem,
            recv_sem=rsem,
            device_id=(to_f, g if to_g is None else to_g),
            device_id_type=MESH,
        )

    even, odd = c == 0, c == 1

    barrier = pltpu.get_barrier_semaphore()
    friends = [(p, g) for p in zpeer[1:]] + [(p, g) for p in qpeer[1:]] + [(f, p) for p in gs[1:]]
    for friend in friends:
        pl.semaphore_signal(barrier, inc=1, device_id=friend, device_id_type=MESH)
    pl.semaphore_wait(barrier, len(friends))

    half = [pl.ds(0, ROWS // 2), pl.ds(ROWS // 2, ROWS // 2)]

    def x_copy(n):
        if n < 4:
            to, part = ((1, 0), (3, 1), (1, 1), (3, 0))[n]
            src, dst = x_ref.at[half[part]], xs.at[g, half[part]]
        elif n == 4:
            to, src = 1, xs.at[gs[3], half[0]]
            dst = src
        else:
            to, src = 3, xs.at[gs[1], half[1]]
            dst = src
        return remote(src, dst, s_x.at[n], r_x.at[n], f, gs[to])

    def x_landed(n):
        block, part = ((3, 0), (1, 1), (3, 1), (1, 0), (2, 0), (2, 1))[n]
        dst = xs.at[gs[block], half[part]]
        remote(dst, dst, s_x.at[n], r_x.at[n], f, gs[1]).wait_recv()

    def gather_sends(k):
        zk = zs[GATHER[k] % NZ]
        both = {}
        for parity in (0, 1):
            unit = tab.at[0, zk] if parity == 0 else tab.at[1, zk, y]
            group = tab.at[parity, zk]
            chain = []
            if -4 < GATHER[k] <= 0:
                chain.append((unit, s_ch.at[k], r_ch.at[k + 2 if k else 1], right))
            if 0 <= GATHER[k] < 3:
                chain.append((unit, s_ch.at[k if k else 8], r_ch.at[k + 2], left))
            spread = []
            if parity == 1:
                spread = [
                    (unit, s_y.at[k, i], r_y.at[k, i], ypeer[i]) for i in range(3)
                ]
            both[parity] = (chain, spread, (group, s_p.at[k], r_p.at[k], mate))
        return both

    def first_spread():
        unit = tab.at[0, z, y]
        return [(unit, s_y.at[0, i], r_y.at[0, i], ypeer[i]) for i in range(3)]

    def go(item):
        unit, ssem, rsem, to = item
        remote(unit, unit, ssem, rsem, to).start()

    def landed(dst, ssem, rsem):
        remote(dst, dst, ssem, rsem, mate).wait_recv()

    def gather_open(own):
        @pl.when(even)
        def _():
            tab[0, z, y] = own
            for item in first_spread():
                go(item)

        @pl.when(odd)
        def _():
            tab[1, z, y] = own

    def gather_comm1(k):
        zk = zs[GATHER[k] % NZ]
        sends = gather_sends(k)

        @pl.when(even)
        def _():
            if k == 0:
                for i, d in enumerate(YD):
                    landed(tab.at[0, z, ys[(NY - d) % NY]], s_y.at[0, i], r_y.at[0, i])
            else:
                landed(tab.at[0, zk], s_ch.at[k], r_ch.at[k])
            chain, _, group = sends[0]
            for item in chain:
                go(item)
            go(group)

        @pl.when(odd)
        def _():
            if k > 0:
                landed(tab.at[1, zk, y], s_ch.at[k], r_ch.at[k])
            chain, spread, _ = sends[1]
            for item in chain + spread:
                go(item)

    def gather_comm2(k):
        zk = zs[GATHER[k] % NZ]
        sends = gather_sends(k)

        @pl.when(odd)
        def _():
            for i, d in enumerate(YD):
                landed(tab.at[1, zk, ys[(NY - d) % NY]], s_y.at[k, i], r_y.at[k, i])
            go(sends[1][2])

    def gather_wait(k):
        landed(tab.at[1 - c, zs[GATHER[k] % NZ]], s_p.at[k], r_p.at[k])

    def gather_drain():
        for parity, mine in ((0, even), (1, odd)):

            @pl.when(mine)
            def _():
                items = first_spread() if parity == 0 else []
                for k in range(8):
                    chain, spread, group = gather_sends(k)[parity]
                    items += chain + spread + [group]
                for unit, ssem, rsem, to in items:
                    remote(unit, unit, ssem, rsem, to).wait_send()

    def pick(k, owners, slots, into):
        zk = zs[GATHER[k] % NZ]
        base = (zk * 8).astype(F32)

        def tile(t, carry):
            rows = pl.ds(pl.multiple_of(t * TILE, TILE), TILE)
            rel = owners[rows, :] - jnp.full((TILE, W), base, F32).astype(BF)
            ones = slots[rows, :]
            parts = []
            for parity in (0, 1):
                for yy in range(NY):
                    wanted = jnp.asarray(yy * 2 + parity, BF)
                    parts.append(jnp.where(rel == wanted, ones, jnp.zeros_like(ones)))
            lhs = jnp.concatenate(parts, axis=1)
            rhs = jnp.concatenate(
                [tab[0, zk].reshape(NY * W, W), tab[1, zk].reshape(NY * W, W)], axis=0
            )
            got = jnp.dot(lhs, rhs, preferred_element_type=F32)
            if k == 0:
                into[rows, :] = got
            else:
                into[rows, :] += got
            return carry

        lax.fori_loop(0, ROWS // TILE, tile, 0)

    def lane_rows(index_ref, i):
        return jnp.broadcast_to(index_ref[i : i + 1, :].astype(F32), (W, W))

    sub = lax.broadcasted_iota(jnp.int32, (W, W), 0)
    lane = lax.broadcasted_iota(jnp.int32, (W, W), 1)
    eye = sub == lane
    subf, lanef = sub.astype(F32), lane.astype(F32)
    ones_w = jnp.ones((W, W), BF)

    def prepare(own_ref, slot_ref, slots, slots_t, owners, owners_t):
        for i in range(ROWS // W):
            span = slice(i * W, (i + 1) * W)
            srow, orow = lane_rows(slot_ref, i), lane_rows(own_ref, i)
            slots_t[:, span] = jnp.where(srow == subf, 1.0, 0.0).astype(BF)
            scol = jnp.dot(
                jnp.where(eye, srow, 0.0).astype(BF), ones_w, preferred_element_type=F32
            )
            slots[span, :] = jnp.where(scol == lanef, 1.0, 0.0).astype(BF)
            ocol = jnp.dot(
                jnp.where(eye, orow, 0.0).astype(BF), ones_w, preferred_element_type=F32
            )
            owners[span, :] = ocol.astype(BF)
            oint = own_ref[i : i + 1, :]
            parity = lax.rem(oint, 2)
            flipped = oint + c * (1 - 2 * parity)
            owners_t[:, span] = jnp.broadcast_to(flipped.astype(F32), (W, W)).astype(BF)

    def reduce_next(j):
        d = REDUCE[j]
        if d > 0:
            return right, (j + 2 if j + 2 < 8 else 7)
        return left, (j + 2 if j + 2 < 7 else 8)

    def reduce_block(j, source, psend, grads):
        tz = zs[REDUCE[j] % NZ]
        owners_t, slots_t = (ot_dim, bt_dim) if grads else (ot_ent, bt_ent)

        def block(yy, carry):
            base = (tz * 8 + yy * 2).astype(F32)
            rel = owners_t[...] - jnp.full((W, ROWS), base, F32).astype(BF)
            ones = slots_t[...]
            zero = jnp.zeros_like(ones)
            lhs = jnp.concatenate(
                [
                    jnp.where(rel == jnp.asarray(0, BF), ones, zero),
                    jnp.where(rel == jnp.asarray(1, BF), ones, zero),
                ],
                axis=0,
            )
            got = jnp.dot(lhs, source[...], preferred_element_type=F32)
            pown[j, yy, 0:W] = got[0:W]
            psend[j, yy, 0:W] = got[W : 2 * W].astype(BF)
            if grads:
                first = tz * 8 + yy * 2
                mine = pl.ds(pl.multiple_of((first + c) * 8, 8), 8)
                other = pl.ds(pl.multiple_of((first + 1 - c) * 8, 8), 8)
                blank = jnp.zeros((8, W), F32)
                for n in range(3):
                    pown[j, yy, W + 8 * n : W + 8 * n + 8] = gw[n, mine, :]
                pown[j, yy, W + 24 : W + 32] = blank
                psend[j, yy, W : W + 16] = jnp.concatenate(
                    [gw[0, other, :], gw[1, other, :]], axis=0
                ).astype(BF)
                psend[j, yy, W + 16 : W + 32] = jnp.concatenate(
                    [gw[2, other, :], blank], axis=0
                ).astype(BF)
            return carry

        lax.fori_loop(0, NY, block, 0)

    def reduce_all(source, psend, precv, ysend, yrecv, zsend, zrecv, res, grads):
        tall = pl.ds(0, EXTRA if grads else W)

        def to_mate(j):
            return remote(psend.at[j], precv.at[j], s_p2.at[j], r_p2.at[j], mate)

        def to_next(j, parity):
            to, slot = reduce_next(j)
            src, dst = zsend.at[j], zrecv.at[slot]
            if parity:
                src, dst = zsend.at[j, 0], zrecv.at[slot, 0]
            return remote(src, dst, s_ch2.at[j], r_ch2.at[slot], to)

        def to_y(j, i):
            return remote(ysend.at[j, i], yrecv.at[j, i], s_y2.at[j, i], r_y2.at[j, i], ypeer[i])

        def from_chain(j, parity):
            slots = [] if j < 2 else ([j] if j < 7 else [7, 8])
            total = None
            for slot in slots:
                dst = zrecv.at[slot, 0] if parity else zrecv.at[slot]
                landed(dst, s_ch2.at[0], r_ch2.at[slot])
                piece = dst[...].astype(F32)
                total = piece if total is None else total + piece
            return total

        def from_y(j):
            total = yown[j, tall]
            for i in range(3):
                landed(yrecv.at[j, i], s_y2.at[j, i], r_y2.at[j, i])
            for i in range(3):
                total = total + yrecv[j, i].astype(F32)
            return total

        def stage1(j):
            landed(precv.at[j], s_p2.at[j], r_p2.at[j])
            pown[j, :, tall] = pown[j, :, tall] + precv[j].astype(F32)

            @pl.when(even)
            def _():
                chain = from_chain(j, 0)
                total = pown[j, :, tall]
                if chain is not None:
                    total = total + chain
                if j < 7:
                    zsend[j] = total.astype(BF)
                    to_next(j, 0).start()
                else:
                    pown[j, :, tall] = total
                    spread_y(j)

            @pl.when(odd)
            def _():
                spread_y(j)

        def spread_y(j):
            for i, d in enumerate(YD):
                ysend[j, i] = pown[j, ys[d], tall].astype(BF)
                to_y(j, i).start()
            yown[j, tall] = pown[j, y, tall]

        def stage2(j):
            @pl.when(odd)
            def _():
                total = from_y(j)
                chain = from_chain(j, 1)
                if chain is not None:
                    total = total + chain
                if j < 7:
                    zsend[j, 0] = total.astype(BF)
                    to_next(j, 1).start()
                else:
                    res[...] = total

            if j == 7:

                @pl.when(even)
                def _():
                    res[...] = from_y(7)

        for step in range(10):
            if step < 8:
                reduce_block(step, source, psend, grads)
                to_mate(step).start()
            if 1 <= step < 9:
                stage1(step - 1)
            if step >= 2:
                stage2(step - 2)

        def drain():
            for j in range(8):
                to_mate(j).wait_send()

            @pl.when(even)
            def _():
                for j in range(7):
                    to_next(j, 0).wait_send()
                for i in range(3):
                    to_y(7, i).wait_send()

            @pl.when(odd)
            def _():
                for j in range(7):
                    to_next(j, 1).wait_send()
                for j in range(8):
                    for i in range(3):
                        to_y(j, i).wait_send()

        return drain

    def small(src, dst, ssem, rsem, i):
        return remote(src, dst, ssem.at[i], rsem.at[i], f, gs[YD[i]])

    def small_landed(dst, ssem, rsem):
        for i, d in enumerate(YD):
            ref = dst(gs[(4 - d) % 4])
            remote(ref, ref, ssem.at[i], rsem.at[i], f, gs[1]).wait_recv()

    def h_copy(i):
        return small(h_ref, hx.at[g], s_h, r_h, i)

    def c_copy(i):
        return small(cot_ref, cx.at[g], s_c, r_c, i)

    def w_copy(i):
        return small(w2.at[c, g], w2.at[c, g], s_w, r_w, i)

    def w_mate(i):
        unit = w2.at[c, gs[(4 - YD[i]) % 4]]
        return remote(unit, unit, s_wp.at[i], r_wp.at[i], mate)

    def a_copy(i):
        return small(ax.at[g], ax.at[g], s_a, r_a, i)

    def n1_copy(d):
        return remote(ch.at[zs[d]], cr1.at[d - 1], s_n1.at[d - 1], r_n1.at[d - 1], zpeer[d])

    def n2_copy(d):
        return remote(cs, cr2.at[d - 1], s_n2.at[d - 1], r_n2.at[d - 1], qpeer[d])

    gather_open(table_ref[...])
    for n in range(4):
        x_copy(n).start()
    gather_comm1(0)
    prepare(dim_own_ref, dim_slot_ref, b_dim, bt_dim, o_dim, ot_dim)
    xs[g] = x_ref[...]
    hx[g] = h_ref[...]
    cx[g] = cot_ref[...]
    w2[0, g] = w_self_ref[...]
    w2[1, g] = w_neigh_ref[...]
    gather_comm1(1)
    gather_comm2(0)
    prepare(ent_own_ref, ent_slot_ref, b_ent, bt_ent, o_ent, ot_ent)

    owner_no = lax.broadcasted_iota(jnp.int32, (64, W), 0).astype(F32)
    hits = jnp.zeros((64, W), F32)
    for i in range(ROWS // W):
        orow = jnp.broadcast_to(ent_own_ref[i : i + 1, :].astype(F32), (64, W))
        named = jnp.where(orow == owner_no, 1.0, 0.0).astype(BF)
        hits = hits + jnp.dot(named, b_ent[i * W : (i + 1) * W, :], preferred_element_type=F32)
    ch[...] = hits.reshape(8, 8, W)
    for d in range(1, 8):
        n1_copy(d).start()

    for step in range(2, 10):
        if step < 8:
            gather_comm1(step)
        if step - 1 < 8:
            gather_comm2(step - 1)
        if step == 5:
            x_landed(0)
            x_copy(4).start()
            x_landed(1)
            x_copy(5).start()
        gather_wait(step - 2)
        pick(step - 2, o_dim, b_dim, acc)

    for n in range(2, 6):
        x_landed(n)
    for i in range(3):
        h_copy(i).start()
        c_copy(i).start()
        w_copy(i).start()

    def message_tile(t, carry):
        rows = pl.ds(pl.multiple_of(t * TILE, TILE), TILE)
        feats = jnp.concatenate([xs[b, rows, :] for b in range(4)], axis=1)
        v = acc[rows, :] + jnp.dot(feats, w_msg_ref[...], preferred_element_type=F32)
        s = sigmoid_of(v)
        val[rows, :] = (v * s).astype(BF)
        slope[rows, :] = s * (1.0 + v * (1.0 - s))
        return carry

    lax.fori_loop(0, ROWS // TILE, message_tile, 0)
    gather_drain()

    for d in range(1, 8):
        ref = cr1.at[d - 1]
        landed(ref, s_n1.at[d - 1], r_n1.at[d - 1])
    zsum = ch[z]
    for d in range(1, 8):
        zsum = zsum + cr1[d - 1]
    cs[...] = zsum
    for d in range(1, 8):
        n2_copy(d).start()

    drain1 = reduce_all(val, psend1, precv1, ysend1, yrecv1, zsend1, zrecv1, res1, False)

    for d in range(1, 8):
        landed(cr2.at[d - 1], s_n2.at[d - 1], r_n2.at[d - 1])
    hsum = cs[...]
    for d in range(1, 8):
        hsum = hsum + cr2[d - 1]
    row_no = lax.broadcasted_iota(jnp.int32, (8, W), 0)
    mine_row = jnp.sum(jnp.where(row_no == q, hsum, 0.0), axis=0, keepdims=True)
    column = jnp.sum(
        jnp.where(eye, jnp.broadcast_to(mine_row, (W, W)), 0.0), axis=1, keepdims=True
    )
    div[...] = jnp.broadcast_to(jnp.maximum(column, 1.0), (W, W))

    ax[g] = (res1[...] / div[...]).astype(BF)
    for i in range(3):
        a_copy(i).start()
    drain1()
    small_landed(lambda b: hx.at[b], s_h, r_h)
    small_landed(lambda b: cx.at[b], s_c, r_c)
    small_landed(lambda b: w2.at[c, b], s_w, r_w)
    for i in range(3):
        w_mate(i).start()
    h_full = jnp.concatenate([hx[b] for b in range(4)], axis=1)
    for i, d in enumerate(YD):
        ref = w2.at[1 - c, gs[(4 - d) % 4]]
        landed(ref, s_wp.at[i], r_wp.at[i])
    for b in range(4):
        pre[b] = jnp.dot(h_full, w2[0, b], preferred_element_type=F32)
    small_landed(lambda b: ax.at[b], s_a, r_a)
    a_full = jnp.concatenate([ax[b] for b in range(4)], axis=1)
    d_agg = jnp.zeros((W, W), F32)
    mine_rows = pl.ds(pl.multiple_of(g * W, W), W)
    for b in range(4):
        v = pre[b] + jnp.dot(a_full, w2[1, b], preferred_element_type=F32)
        pre[b] = v
        s = sigmoid_of(v)
        d_pre = (cx[b].astype(F32) * (s * (1.0 + v * (1.0 - s)))).astype(BF)
        d_agg = d_agg + lax.dot_general(
            d_pre, w2[1, b, mine_rows, :], (((1,), (1,)), ((), ())), preferred_element_type=F32
        )
    gather_open((d_agg / div[...]).astype(BF))
    gather_comm1(0)
    v = pre[g]
    s = sigmoid_of(v)
    out_ref[...] = (v * s).astype(BF)
    d_pre = (cot_ref[...].astype(F32) * (s * (1.0 + v * (1.0 - s)))).astype(BF)
    for b in range(4):
        span = slice(b * W, (b + 1) * W)
        gw[1, span, :] = lax.dot_general(
            hx[b], d_pre, (((0,), (0,)), ((), ())), preferred_element_type=F32
        )
        gw[2, span, :] = lax.dot_general(
            ax[b], d_pre, (((0,), (0,)), ((), ())), preferred_element_type=F32
        )

    for step in range(1, 10):
        if step < 8:
            gather_comm1(step)
        if 0 <= step - 1 < 8:
            gather_comm2(step - 1)
        if step >= 2:
            gather_wait(step - 2)
            pick(step - 2, o_ent, b_ent, dmsg)

    def back_tile(t, carry):
        rows = pl.ds(pl.multiple_of(t * TILE, TILE), TILE)
        val[rows, :] = (dmsg[rows, :] * slope[rows, :]).astype(BF)
        return carry

    lax.fori_loop(0, ROWS // TILE, back_tile, 0)
    gather_drain()
    for b in range(4):
        gw[0, b * W : (b + 1) * W, :] = lax.dot_general(
            xs[b], val[...], (((0,), (0,)), ((), ())), preferred_element_type=F32
        )
    drain2 = reduce_all(val, psend2, precv2, ysend2, yrecv2, zsend2, zrecv2, res2, True)
    gdim_ref[...] = res2[0:W]
    gwm_ref[...] = res2[W : W + 8]
    gws_ref[...] = res2[W + 8 : W + 16]
    gwn_ref[...] = res2[W + 16 : W + 24]

    drain2()
    for n in range(6):
        x_copy(n).wait_send()
    for i in range(3):
        h_copy(i).wait_send()
        c_copy(i).wait_send()
        w_copy(i).wait_send()
        w_mate(i).wait_send()
        a_copy(i).wait_send()
    for d in range(1, 8):
        n1_copy(d).wait_send()
        n2_copy(d).wait_send()


def shards(x, dim_owner, dim_slot, fact_owner, fact_slot, table, h, w_msg, w_self, w_neigh, cot):
    tile = (ROWS // W, W)
    vmem = pl.BlockSpec(memory_space=pltpu.VMEM)
    dma = pltpu.SemaphoreType.DMA

    def lots(tall, *lead):
        return pltpu.VMEM((*lead, tall, W), BF)

    def stages(tall):
        return [
            lots(tall, 8, NY),
            lots(tall, 8, NY),
            lots(tall, 8, 3),
            lots(tall, 8, 3),
            lots(tall, 8, NY),
            lots(tall, 9, NY),
        ]

    def sems(*shape):
        return [dma(shape), dma(shape)]

    scratch = [
        lots(ROWS, 4),
        lots(W, 2, NZ, NY),
        pltpu.VMEM((ROWS, W), BF),
        pltpu.VMEM((ROWS, W), BF),
        pltpu.VMEM((W, ROWS), BF),
        pltpu.VMEM((W, ROWS), BF),
        pltpu.VMEM((ROWS, W), BF),
        pltpu.VMEM((ROWS, W), BF),
        pltpu.VMEM((W, ROWS), BF),
        pltpu.VMEM((W, ROWS), BF),
        pltpu.VMEM((ROWS, W), F32),
        pltpu.VMEM((ROWS, W), F32),
        pltpu.VMEM((ROWS, W), F32),
        pltpu.VMEM((ROWS, W), BF),
        pltpu.VMEM((8, 8, W), F32),
        pltpu.VMEM((8, W), F32),
        pltpu.VMEM((7, 8, W), F32),
        pltpu.VMEM((7, 8, W), F32),
        lots(W, 4),
        lots(W, 4),
        lots(W, 4),
        lots(512, 2, 4),
        pltpu.VMEM((4, W, W), F32),
        pltpu.VMEM((3, 512, W), F32),
        pltpu.VMEM((8, NY, EXTRA, W), F32),
        pltpu.VMEM((8, EXTRA, W), F32),
        *stages(W),
        *stages(EXTRA),
        pltpu.VMEM((W, W), F32),
        pltpu.VMEM((EXTRA, W), F32),
        pltpu.VMEM((W, W), F32),
        *sems(9),
        *sems(8, 3),
        *sems(8),
        *sems(9),
        *sems(8, 3),
        *sems(8),
        *sems(6),
        *sems(3),
        *sems(3),
        *sems(3),
        *sems(3),
        *sems(3),
        *sems(7),
        *sems(7),
    ]
    return pl.pallas_call(
        kernel,
        out_shape=(
            jax.ShapeDtypeStruct((W, W), BF),
            jax.ShapeDtypeStruct((8, W), F32),
            jax.ShapeDtypeStruct((8, W), F32),
            jax.ShapeDtypeStruct((8, W), F32),
            jax.ShapeDtypeStruct((W, W), F32),
        ),
        in_specs=[vmem] * 11,
        out_specs=(vmem,) * 5,
        scratch_shapes=scratch,
        compiler_params=pltpu.CompilerParams(
            collective_id=0, has_side_effects=True, vmem_limit_bytes=56 * 1024 * 1024
        ),
    )(
        x,
        dim_owner.reshape(tile),
        dim_slot.reshape(tile),
        fact_owner.reshape(tile),
        fact_slot.reshape(tile),
        table,
        h,
        w_msg,
        w_self,
        w_neigh,
        cot,
    )


def solution(mesh):
    placed = (
        P("fact", "feat"),
        P("fact", None),
        P("fact"),
        P("fact", None),
        P("fact"),
        P("fact", "feat"),
        P("fact", "feat"),
        P(None, "feat"),
        P(None, "feat"),
        P(None, "feat"),
        P("fact", "feat"),
    )
    return jax.shard_map(
        shards,
        mesh=mesh,
        in_specs=placed,
        out_specs=(P("fact", "feat"),) * 5,
        check_vma=False,
    )
```

time: 921 us -> 121 us (0.13)
  waiting for transfers between devices: 482 us -> 0 us
  blocking collectives: 267 us -> 0 us
  Pallas kernels: 0 us -> 116 us
  matrix products: 61.8 us -> 0 us
  loops' own time: 52.5 us -> 0 us
  local copies, waits for them, and re-layouts: 28 us -> 3.98 us
  between operations: 15.6 us -> 0.67 us
  other arithmetic: 11.6 us -> 0 us
    unnamed x1 -> x0, blocking collectives: 245 us -> none
    reduce_scatter x3 -> x0, waiting for transfers between devices: 169 us -> none  [the longest x1 144 us: shards(): lax.psum_scatter(sum_rows(fact_dim, d_msgpre, dim_local * lax.axis_size('...]
    unnamed x8 -> x0, waiting for transfers between devices: 158 us -> none
    all_gather x3 -> x0, waiting for transfers between devices: 154 us -> none  [the longest x1 78.5 us: shards(): lax.all_gather(dim_table, 'fact', axis=0, tiled=True)]
    pallas_call x0 -> x1, Pallas kernels: none -> 116 us  [shards(): pl.pallas_call(kernel, out_shape=(jax.ShapeDtypeStruct((W, W), BF), jax.S...]
    dot_general x39 -> x0, matrix products: 61.8 us -> none  [the longest x16 30 us: advance(): jnp.dot(selector, block, preferred_element_type=jnp.float32)]
    another operation x4 -> x0, loops' own time: 52.5 us -> none  [the longest x2 42 us: pick_rows(): lax.scan(advance, initial, jnp.arange(num_blocks, dtype=jnp.int32))]
    all_gather x2 -> x0, blocking collectives: 22.2 us -> none  [the longest x1 11.5 us: shards(): lax.all_gather(entity_h, 'feat', axis=1, tiled=True)]
  transfers between devices with their start and end apart: 7 -> 0, of which waited for: 5 -> 0; matrix products, arithmetic and copies ran while one was open for 6% -> 0% of each run, Pallas kernels for 0% -> 0%
where the time goes in v1:
time: 121 us; the launch traced here: 120 us
  Pallas kernels  116 us (96%)
  local copies, waits for them, and re-layouts  3.98 us (3%)
    pallas_call x1, Pallas kernels, shards(): pl.pallas_call(kernel, out_shape=(jax.ShapeDtypeStruct((W, W), BF), jax.S...  116 us
    unnamed x13, local copies, waits for them, and re-layouts  3.98 us

profile of v1, /device:TPU:8, one launch (start us, length us, event | category | flops | bytes accessed | tf_op | source)
XLA Modules:
  0.0 120.4 jit_solution(2277413337562967606)
XLA Ops:
  0.6 115.8 %shard_map.146 = (bf16[128,128]{1,0:T(8,128)(2,1)}, f32[8,128]{1,0:T(8,128)}, f32[8,128]{1,0:T(8,128)}, f32[8,128]{1,0:T(8,128)}, f32[128,128]{1,0:T(8,128)}) custom-call(bf16[1024,128]{1,0:T(8,128)(2,1)} %x_ref.1, s32[8,128]{1,0:T(8,128)} %bitcast.4, s32[8,128]{1,0:T(8,128)} %bitcast.5, s32[8,128]{1,0:T(8,128)} %bitcast.6, s32[8,128]{1,0:T(8,128)} %bitcast.7, ...), custom_call_target="tpu_custom_call" | custom-call | tf_op jit(solution)/shard_map/pallas_call | solution.py:724
  116.4 0.0 copy-start
  116.4 0.0 copy-start.3
  116.4 1.4 %copy.21 = bf16[128,128]{1,0:T(8,128)(2,1)} copy(bf16[128,128]{1,0:T(8,128)(2,1)} %get-tuple-element.10) | data formatting | bytes 65536
  117.8 0.0 copy-done.3
  117.8 0.0 copy-start.2
  117.8 0.6 copy.22
  118.4 0.1 copy-done.2
  118.5 0.0 copy-start.1
  118.5 0.6 copy.23
  119.1 0.1 copy-done.1
  119.2 0.6 copy.24
  119.8 0.0 copy-done
  119.8 0.6 copy.25
Async XLA Ops:
  116.4 3.4 %copy-start = (f32[128,128]{1,0:T(8,128)S(1)}, f32[128,128]{1,0:T(8,128)}, u32[]{:S(2)}) copy-start(f32[128,128]{1,0:T(8,128)} %get-tuple-element.14) | copy-start | bytes 196612
  116.4 1.4 %copy-start.3 = (f32[8,128]{1,0:T(8,128)S(1)}, f32[8,128]{1,0:T(8,128)}, u32[]{:S(2)}) copy-start(f32[8,128]{1,0:T(8,128)} %get-tuple-element.11) | copy-start | bytes 12292
  117.8 0.7 copy-start.2
  118.5 0.7 copy-start.1

commit v2 on v1

v2 whole, which is shorter than its diff:
```python
import jax
import jax.numpy as jnp
from jax import lax
from jax.experimental import pallas as pl
from jax.experimental.pallas import tpu as pltpu
from jax.sharding import PartitionSpec as P

MESH = pl.DeviceIdType.MESH
BF = jnp.bfloat16
F32 = jnp.float32

NZ, NY = 8, 4
EVENTS = (0, -2, 2, -3, 3, 4, -1, 1)
FAR = 6
TARGETS = (4, -3, 1, -1, 3, -2, 2, 0)
NEAR_AT = (2, 3)
FAR_AT = (0, 1, 4, 5, 6)
YD = (1, 3, 2)
ROWS = 1024
TILE = 256
W = 128
EXTRA = 160
LAG = 5


def sigmoid_of(v):
    return 1.0 / (1.0 + jnp.exp(-v))


def kernel(
    x_ref,
    dim_own_ref,
    dim_slot_ref,
    ent_own_ref,
    ent_slot_ref,
    table_ref,
    h_ref,
    w_msg_ref,
    w_self_ref,
    w_neigh_ref,
    cot_ref,
    out_ref,
    sums_ref,
    xs,
    tab,
    b_ent,
    bt_dim,
    bt_ent,
    ot_dim,
    ot_ent,
    acc,
    slope,
    val,
    ch,
    cs,
    cr1,
    cr2,
    hx,
    cx,
    ax,
    w2,
    wm,
    pre,
    gw,
    pown,
    yown,
    psend1,
    precv1,
    gsend1,
    grecv1,
    ysend1,
    yrecv1,
    zsend1,
    zrecv1,
    psend2,
    precv2,
    gsend2,
    grecv2,
    ysend2,
    yrecv2,
    zsend2,
    zrecv2,
    res1,
    res2,
    div,
    s_ch,
    r_ch,
    s_y,
    r_y,
    s_p,
    r_p,
    s_ch2,
    r_ch2,
    s_y2,
    r_y2,
    s_p2,
    r_p2,
    s_x,
    r_x,
    s_h,
    r_h,
    s_c,
    r_c,
    s_w,
    r_w,
    s_wp,
    r_wp,
    s_a,
    r_a,
    s_n1,
    r_n1,
    s_n2,
    r_n2,
    s_in,
    keys_v,
    keys_dim,
    keys_ent,
    wide,
):
    f = lax.axis_index("fact")
    g = lax.axis_index("feat")
    z, y, c = f // 8, lax.rem(f // 2, 4), lax.rem(f, 2)
    q = lax.rem(f, 8)

    def at(zz, yy, cc):
        return (zz * 4 + yy) * 2 + cc

    zs = [lax.rem(z + d, NZ) for d in range(NZ)]
    ys = [lax.rem(y + d, NY) for d in range(NY)]
    gs = [lax.rem(g + d, 4) for d in range(4)]
    right, left, mate = at(zs[1], y, c), at(zs[7], y, c), at(z, y, 1 - c)
    zpeer = [at(zs[d], y, c) for d in range(NZ)]
    ypeer = [at(z, ys[d], c) for d in YD]
    qpeer = [z * 8 + lax.rem(q + d, 8) for d in range(8)]

    def remote(src, dst, ssem, rsem, to_f, to_g=None):
        return pltpu.make_async_remote_copy(
            src_ref=src,
            dst_ref=dst,
            send_sem=ssem,
            recv_sem=rsem,
            device_id=(to_f, g if to_g is None else to_g),
            device_id_type=MESH,
        )

    barrier = pltpu.get_barrier_semaphore()
    friends = [(p, g) for p in zpeer[1:]] + [(p, g) for p in qpeer[1:]] + [(f, p) for p in gs[1:]]
    for friend in friends:
        pl.semaphore_signal(barrier, inc=1, device_id=friend, device_id_type=MESH)

    half = [pl.ds(0, ROWS // 2), pl.ds(ROWS // 2, ROWS // 2)]

    def x_copy(n):
        if n < 4:
            to, part = ((1, 0), (3, 1), (1, 1), (3, 0))[n]
            src = xs.at[g, half[part]]
            dst = src
        elif n == 4:
            to, src = 1, xs.at[gs[3], half[0]]
            dst = src
        else:
            to, src = 3, xs.at[gs[1], half[1]]
            dst = src
        return remote(src, dst, s_x.at[n], r_x.at[n], f, gs[to])

    def x_landed(n):
        block, part = ((3, 0), (1, 1), (3, 1), (1, 0), (2, 0), (2, 1))[n]
        dst = xs.at[gs[block], half[part]]
        remote(dst, dst, s_x.at[n], r_x.at[n], f, gs[1]).wait_recv()

    def unit(k):
        return tab.at[c, zs[EVENTS[k] % NZ], y]

    def group(k):
        return tab.at[c, zs[EVENTS[k] % NZ]]

    def z_send(k):
        piece = unit(0) if k < FAR else group(0)
        return remote(piece, piece, s_ch.at[k], r_ch.at[k], zpeer[-EVENTS[k] % NZ])

    def y_send(k, i):
        return remote(unit(k), unit(k), s_y.at[k, i], r_y.at[k, i], ypeer[i])

    def p_send(k):
        return remote(group(k), group(k), s_p.at[k], r_p.at[k], mate)

    def landed(dst, ssem, rsem):
        remote(dst, dst, ssem, rsem, mate).wait_recv()

    def gather_open():
        for k in range(1, FAR):
            z_send(k).start()
        for i in range(3):
            y_send(0, i).start()

    def gather_near():
        gather_join(0)
        for k in (6, 7):
            z_send(k).start()

    def gather_spread(k):
        landed(unit(k), s_ch.at[k], r_ch.at[k])
        for i in range(3):
            y_send(k, i).start()

    def gather_join(k):
        zk = zs[EVENTS[k] % NZ]
        if k < FAR:
            for i, d in enumerate(YD):
                landed(tab.at[c, zk, ys[(NY - d) % NY]], s_y.at[k, i], r_y.at[k, i])
        else:
            landed(group(k), s_ch.at[k], r_ch.at[k])
        p_send(k).start()

    def gather_drain():
        for k in range(8):
            if k > 0:
                z_send(k).wait_send()
            if k < FAR:
                for i in range(3):
                    y_send(k, i).wait_send()
            p_send(k).wait_send()

    def gather_run(keys, sink, hooks):
        def use(k):
            zk = zs[EVENTS[k] % NZ]
            landed(tab.at[1 - c, zk], s_p.at[k], r_p.at[k])
            for parity in (0, 1):
                first = parity * NZ * NY * W + zk * (NY * W)
                rows = pl.ds(pl.multiple_of(first, NY * W), NY * W)
                wide[rows, :] = tab[parity, zk].reshape(NY * W, W).astype(F32)

        plan = (
            (gather_spread, 1),
            (gather_spread, 2),
            (use, 0),
            (gather_spread, 3),
            (gather_spread, 4),
            (gather_spread, 5),
            (gather_join, 1),
            (gather_join, 2),
            (gather_join, 6),
            (gather_join, 7),
            (gather_join, 3),
            (gather_join, 4),
            (use, 1),
            (use, 2),
            (use, 6),
            (use, 7),
            (gather_join, 5),
            (use, 3),
            (use, 4),
            (use, 5),
        )
        for n, (stage, k) in enumerate(plan):
            if n in hooks:
                hooks[n]()
            stage(k)

        def some(t, carry):
            i, first = t // 4, lax.rem(t, 4) * 32
            found = [wide[pl.ds(keys[i, first + j], 1), :] for j in range(32)]
            sink(pl.ds(pl.multiple_of(t * 32, 32), 32), jnp.concatenate(found, axis=0))
            return carry

        lax.fori_loop(0, ROWS // 32, some, 0)

    def key_tile(own_ref, slot_ref):
        owns = own_ref[...]
        return lax.rem(owns, 2) * (NZ * NY * W) + (owns // 2) * W + slot_ref[...]

    def lane_rows(index_ref, i):
        return jnp.broadcast_to(index_ref[i : i + 1, :].astype(F32), (W, W))

    sub = lax.broadcasted_iota(jnp.int32, (W, W), 0)
    lane = lax.broadcasted_iota(jnp.int32, (W, W), 1)
    eye = sub == lane
    subf, lanef = sub.astype(F32), lane.astype(F32)
    ones_w = jnp.ones((W, W), BF)

    def prepare(own_ref, slot_ref, slots, slots_t, owners_t):
        for i in range(ROWS // W):
            span = slice(i * W, (i + 1) * W)
            srow = lane_rows(slot_ref, i)
            slots_t[:, span] = jnp.where(srow == subf, 1.0, 0.0).astype(BF)
            if slots is not None:
                scol = jnp.dot(
                    jnp.where(eye, srow, 0.0).astype(BF), ones_w, preferred_element_type=F32
                )
                slots[span, :] = jnp.where(scol == lanef, 1.0, 0.0).astype(BF)
            oint = own_ref[i : i + 1, :]
            flipped = oint + c * (1 - 2 * lax.rem(oint, 2))
            owners_t[:, span] = jnp.broadcast_to(flipped.astype(F32), (W, W)).astype(BF)

    def reduce_block(j, source, psend, grads):
        tz = zs[TARGETS[j] % NZ]
        owners_t, slots_t = (ot_dim, bt_dim) if grads else (ot_ent, bt_ent)

        base = (tz * 8).astype(F32)
        rel = owners_t[...] - jnp.full((W, ROWS), base, F32).astype(BF)
        ones = slots_t[...]
        zero = jnp.zeros_like(ones)
        lhs = jnp.concatenate(
            [
                jnp.where(rel == jnp.asarray(yy * 2 + side, BF), ones, zero)
                for side in (1, 0)
                for yy in range(NY)
            ],
            axis=0,
        )
        got = jnp.dot(lhs, source[...], preferred_element_type=F32)
        for yy in range(NY):
            psend[j, yy, 0:W] = got[yy * W : (yy + 1) * W].astype(BF)
            pown[j, yy, 0:W] = got[(NY + yy) * W : (NY + yy + 1) * W]
        if grads:
            blank = jnp.zeros((8, W), F32)
            for yy in range(NY):
                first = tz * 8 + yy * 2
                mine = pl.ds(pl.multiple_of((first + c) * 8, 8), 8)
                other = pl.ds(pl.multiple_of((first + 1 - c) * 8, 8), 8)
                for n in range(3):
                    pown[j, yy, W + 8 * n : W + 8 * n + 8] = gw[n, mine, :]
                pown[j, yy, W + 24 : W + 32] = blank
                psend[j, yy, W : W + 16] = jnp.concatenate(
                    [gw[0, other, :], gw[1, other, :]], axis=0
                ).astype(BF)
                psend[j, yy, W + 16 : W + 32] = jnp.concatenate(
                    [gw[2, other, :], blank], axis=0
                ).astype(BF)

    def reduce_all(
        source, psend, precv, gsend, grecv, ysend, yrecv, zsend, zrecv, res, grads, hooks
    ):
        tall = pl.ds(0, EXTRA if grads else W)

        def to_mate(j):
            return remote(psend.at[j], precv.at[j], s_p2.at[j], r_p2.at[j], mate)

        def slot(j):
            return 5 if j == 7 else FAR_AT.index(j)

        def to_y(j, i):
            n = slot(j)
            return remote(ysend.at[n, i], yrecv.at[n, i], s_y2.at[n, i], r_y2.at[n, i], ypeer[i])

        def to_z(j):
            to = zpeer[TARGETS[j] % NZ]
            if j in NEAR_AT:
                n = NEAR_AT.index(j)
                return remote(gsend.at[n], grecv.at[n], s_ch2.at[j], r_ch2.at[j], to)
            n = slot(j)
            return remote(zsend.at[n], zrecv.at[n], s_ch2.at[j], r_ch2.at[j], to)

        def stage1(j):
            landed(precv.at[j], s_p2.at[j], r_p2.at[j])
            if j in NEAR_AT:
                gsend[NEAR_AT.index(j)] = (pown[j, :, tall] + precv[j].astype(F32)).astype(BF)
                to_z(j).start()
                return
            if j == 7:
                for n in range(2):
                    landed(grecv.at[n], s_ch2.at[NEAR_AT[n]], r_ch2.at[NEAR_AT[n]])

            def block(yy):
                got = pown[j, yy, tall] + precv[j, yy].astype(F32)
                if j == 7:
                    for n in range(2):
                        got = got + grecv[n, yy].astype(F32)
                return got

            for i, d in enumerate(YD):
                ysend[slot(j), i] = block(ys[d]).astype(BF)
                to_y(j, i).start()
            yown[j, tall] = block(y)

        def stage2(j):
            for i in range(3):
                n = slot(j)
                landed(yrecv.at[n, i], s_y2.at[n, i], r_y2.at[n, i])
            total = yown[j, tall]
            for i in range(3):
                total = total + yrecv[slot(j), i].astype(F32)
            if j < 7:
                zsend[slot(j)] = total.astype(BF)
                to_z(j).start()
            else:
                res[...] = total

        for step in range(8 + LAG):
            if step < 8:
                reduce_block(step, source, psend, grads)
                to_mate(step).start()
            if 1 <= step < 9:
                stage1(step - 1)
            if step in hooks:
                hooks[step]()
            if step >= LAG and step - LAG not in NEAR_AT:
                stage2(step - LAG)

        for n, j in enumerate(FAR_AT):
            landed(zrecv.at[n], s_ch2.at[j], r_ch2.at[j])
        total = res[...]
        for n in range(5):
            total = total + zrecv[n].astype(F32)
        res[...] = total

        def drain():
            for j in range(8):
                to_mate(j).wait_send()
                if j not in NEAR_AT:
                    for i in range(3):
                        to_y(j, i).wait_send()
                if j < 7:
                    to_z(j).wait_send()

        return drain

    def small(src, dst, ssem, rsem, i):
        return remote(src, dst, ssem.at[i], rsem.at[i], f, gs[YD[i]])

    def small_landed(dst, ssem, rsem):
        for i, d in enumerate(YD):
            ref = dst(gs[(4 - d) % 4])
            remote(ref, ref, ssem.at[i], rsem.at[i], f, gs[1]).wait_recv()

    def h_copy(i):
        return small(hx.at[g], hx.at[g], s_h, r_h, i)

    def c_copy(i):
        return small(cx.at[g], cx.at[g], s_c, r_c, i)

    def w_copy(i):
        return small(w2.at[c, g], w2.at[c, g], s_w, r_w, i)

    def w_mate(i):
        unit = w2.at[c, gs[(4 - YD[i]) % 4]]
        return remote(unit, unit, s_wp.at[i], r_wp.at[i], mate)

    def a_copy(i):
        return small(ax.at[g], ax.at[g], s_a, r_a, i)

    def n1_copy(d):
        return remote(ch.at[zs[d]], cr1.at[d - 1], s_n1.at[d - 1], r_n1.at[d - 1], zpeer[d])

    def n2_copy(d):
        return remote(cs, cr2.at[d - 1], s_n2.at[d - 1], r_n2.at[d - 1], qpeer[d])

    inputs = [
        pltpu.make_async_copy(src, dst, s_in.at[n])
        for n, (src, dst) in enumerate(
            (
                (table_ref, tab.at[c, z, y]),
                (x_ref, xs.at[g]),
                (h_ref, hx.at[g]),
                (cot_ref, cx.at[g]),
                (w_self_ref, w2.at[0, g]),
                (w_neigh_ref, w2.at[1, g]),
                (w_msg_ref, wm),
            )
        )
    ]
    for copy in inputs:
        copy.start()
    keys_v[0] = key_tile(dim_own_ref, dim_slot_ref)
    keys_v[1] = key_tile(ent_own_ref, ent_slot_ref)
    to_keys = [
        pltpu.make_async_copy(keys_v.at[0], keys_dim, s_in.at[7]),
        pltpu.make_async_copy(keys_v.at[1], keys_ent, s_in.at[8]),
    ]
    for copy in to_keys:
        copy.start()
    prepare(dim_own_ref, dim_slot_ref, None, bt_dim, ot_dim)
    prepare(ent_own_ref, ent_slot_ref, b_ent, bt_ent, ot_ent)
    owner_no = lax.broadcasted_iota(jnp.int32, (64, W), 0).astype(F32)
    hits = jnp.zeros((64, W), F32)
    for i in range(ROWS // W):
        orow = jnp.broadcast_to(ent_own_ref[i : i + 1, :].astype(F32), (64, W))
        named = jnp.where(orow == owner_no, 1.0, 0.0).astype(BF)
        hits = hits + jnp.dot(named, b_ent[i * W : (i + 1) * W, :], preferred_element_type=F32)
    ch[...] = hits.reshape(8, 8, W)
    for copy in inputs + to_keys:
        copy.wait()
    pl.semaphore_wait(barrier, len(friends))
    gather_open()
    for n in range(2):
        x_copy(n).start()
    for n in range(2):
        x_copy(n).wait_send()
        x_copy(n + 2).start()
    gather_near()
    for d in range(1, 8):
        n1_copy(d).start()

    def relay_x():
        x_landed(0)
        x_copy(4).start()
        x_landed(1)
        x_copy(5).start()

    def keep(rows, found):
        acc[rows, :] = found

    gather_run(keys_dim, keep, {0: relay_x})

    for n in range(2, 6):
        x_landed(n)
    for i in range(3):
        h_copy(i).start()
        c_copy(i).start()
        w_copy(i).start()

    def message_tile(t, carry):
        rows = pl.ds(pl.multiple_of(t * TILE, TILE), TILE)
        feats = jnp.concatenate([xs[b, rows, :] for b in range(4)], axis=1)
        v = acc[rows, :] + jnp.dot(feats, wm[...], preferred_element_type=F32)
        s = sigmoid_of(v)
        val[rows, :] = (v * s).astype(BF)
        slope[rows, :] = s * (1.0 + v * (1.0 - s))
        return carry

    lax.fori_loop(0, ROWS // TILE, message_tile, 0)
    gather_drain()

    for d in range(1, 8):
        ref = cr1.at[d - 1]
        landed(ref, s_n1.at[d - 1], r_n1.at[d - 1])
    zsum = ch[z]
    for d in range(1, 8):
        zsum = zsum + cr1[d - 1]
    cs[...] = zsum
    for d in range(1, 8):
        n2_copy(d).start()

    def weights_on():
        small_landed(lambda b: w2.at[c, b], s_w, r_w)
        for i in range(3):
            w_mate(i).start()

    def from_entities():
        small_landed(lambda b: hx.at[b], s_h, r_h)
        small_landed(lambda b: cx.at[b], s_c, r_c)
        for i, d in enumerate(YD):
            ref = w2.at[1 - c, gs[(4 - d) % 4]]
            landed(ref, s_wp.at[i], r_wp.at[i])
        h_full = jnp.concatenate([hx[b] for b in range(4)], axis=1)
        for b in range(4):
            pre[b] = jnp.dot(h_full, w2[0, b], preferred_element_type=F32)

    drain1 = reduce_all(
        val,
        psend1,
        precv1,
        gsend1,
        grecv1,
        ysend1,
        yrecv1,
        zsend1,
        zrecv1,
        res1,
        False,
        {8: weights_on, 10: from_entities},
    )

    for d in range(1, 8):
        landed(cr2.at[d - 1], s_n2.at[d - 1], r_n2.at[d - 1])
    hsum = cs[...]
    for d in range(1, 8):
        hsum = hsum + cr2[d - 1]
    row_no = lax.broadcasted_iota(jnp.int32, (8, W), 0)
    mine_row = jnp.sum(jnp.where(row_no == q, hsum, 0.0), axis=0, keepdims=True)
    column = jnp.sum(
        jnp.where(eye, jnp.broadcast_to(mine_row, (W, W)), 0.0), axis=1, keepdims=True
    )
    div[...] = jnp.broadcast_to(jnp.maximum(column, 1.0), (W, W))

    ax[g] = (res1[...] / div[...]).astype(BF)
    for i in range(3):
        a_copy(i).start()
    drain1()
    small_landed(lambda b: ax.at[b], s_a, r_a)
    a_full = jnp.concatenate([ax[b] for b in range(4)], axis=1)
    d_agg = jnp.zeros((W, W), F32)
    mine_rows = pl.ds(pl.multiple_of(g * W, W), W)
    for b in range(4):
        v = pre[b] + jnp.dot(a_full, w2[1, b], preferred_element_type=F32)
        pre[b] = v
        s = sigmoid_of(v)
        d_pre = (cx[b].astype(F32) * (s * (1.0 + v * (1.0 - s)))).astype(BF)
        d_agg = d_agg + lax.dot_general(
            d_pre, w2[1, b, mine_rows, :], (((1,), (1,)), ((), ())), preferred_element_type=F32
        )
    tab[c, z, y] = (d_agg / div[...]).astype(BF)
    gather_open()
    v = pre[g]
    s = sigmoid_of(v)
    out_ref[...] = (v * s).astype(BF)
    d_pre = (cx[g].astype(F32) * (s * (1.0 + v * (1.0 - s)))).astype(BF)
    for b in range(4):
        span = slice(b * W, (b + 1) * W)
        gw[1, span, :] = lax.dot_general(
            hx[b], d_pre, (((0,), (0,)), ((), ())), preferred_element_type=F32
        )
        gw[2, span, :] = lax.dot_general(
            ax[b], d_pre, (((0,), (0,)), ((), ())), preferred_element_type=F32
        )

    gather_near()
    def back(rows, found):
        val[rows, :] = (found * slope[rows, :]).astype(BF)

    gather_run(keys_ent, back, {})
    gather_drain()
    for b in range(4):
        gw[0, b * W : (b + 1) * W, :] = lax.dot_general(
            xs[b], val[...], (((0,), (0,)), ((), ())), preferred_element_type=F32
        )
    drain2 = reduce_all(
        val,
        psend2,
        precv2,
        gsend2,
        grecv2,
        ysend2,
        yrecv2,
        zsend2,
        zrecv2,
        res2,
        True,
        {},
    )
    sums_ref[...] = res2[...]

    drain2()
    for n in range(2, 6):
        x_copy(n).wait_send()
    for i in range(3):
        h_copy(i).wait_send()
        c_copy(i).wait_send()
        w_copy(i).wait_send()
        w_mate(i).wait_send()
        a_copy(i).wait_send()
    for d in range(1, 8):
        n1_copy(d).wait_send()
        n2_copy(d).wait_send()


def hand_out(out_in, sums_in, out_ref, gwm_ref, gws_ref, gwn_ref, gdim_ref):
    out_ref[...] = out_in[...]
    gdim_ref[...] = sums_in[0:W]
    gwm_ref[...] = sums_in[W : W + 8]
    gws_ref[...] = sums_in[W + 8 : W + 16]
    gwn_ref[...] = sums_in[W + 16 : W + 24]


def shards(x, dim_owner, dim_slot, fact_owner, fact_slot, table, h, w_msg, w_self, w_neigh, cot):
    tile = (ROWS // W, W)
    vmem = pl.BlockSpec(memory_space=pltpu.VMEM)
    anywhere = pl.BlockSpec(memory_space=pl.ANY)
    dma = pltpu.SemaphoreType.DMA

    def lots(tall, *lead):
        return pltpu.VMEM((*lead, tall, W), BF)

    def stages(tall):
        return [
            lots(tall, 8, NY),
            lots(tall, 8, NY),
            lots(tall, 2, NY),
            lots(tall, 2, NY),
            lots(tall, 6, 3),
            lots(tall, 6, 3),
            lots(tall, 5),
            lots(tall, 5),
        ]

    def sems(*shape):
        return [dma(shape), dma(shape)]

    scratch = [
        lots(ROWS, 4),
        lots(W, 2, NZ, NY),
        pltpu.VMEM((ROWS, W), BF),
        pltpu.VMEM((W, ROWS), BF),
        pltpu.VMEM((W, ROWS), BF),
        pltpu.VMEM((W, ROWS), BF),
        pltpu.VMEM((W, ROWS), BF),
        pltpu.VMEM((ROWS, W), F32),
        pltpu.VMEM((ROWS, W), F32),
        pltpu.VMEM((ROWS, W), BF),
        pltpu.VMEM((8, 8, W), F32),
        pltpu.VMEM((8, W), F32),
        pltpu.VMEM((7, 8, W), F32),
        pltpu.VMEM((7, 8, W), F32),
        lots(W, 4),
        lots(W, 4),
        lots(W, 4),
        lots(512, 2, 4),
        lots(512),
        pltpu.VMEM((4, W, W), F32),
        pltpu.VMEM((3, 512, W), F32),
        pltpu.VMEM((8, NY, EXTRA, W), F32),
        pltpu.VMEM((8, EXTRA, W), F32),
        *stages(W),
        *stages(EXTRA),
        pltpu.VMEM((W, W), F32),
        pltpu.VMEM((EXTRA, W), F32),
        pltpu.VMEM((W, W), F32),
        *sems(9),
        *sems(8, 3),
        *sems(8),
        *sems(9),
        *sems(8, 3),
        *sems(8),
        *sems(6),
        *sems(3),
        *sems(3),
        *sems(3),
        *sems(3),
        *sems(3),
        *sems(7),
        *sems(7),
        dma((9,)),
        pltpu.VMEM((2, ROWS // W, W), jnp.int32),
        pltpu.SMEM((ROWS // W, W), jnp.int32),
        pltpu.SMEM((ROWS // W, W), jnp.int32),
        pltpu.VMEM((2 * NZ * NY * W, W), F32),
    ]
    out, sums = pl.pallas_call(
        kernel,
        out_shape=(
            jax.ShapeDtypeStruct((W, W), BF),
            jax.ShapeDtypeStruct((EXTRA, W), F32),
        ),
        in_specs=[anywhere] + [vmem] * 4 + [anywhere] * 6,
        out_specs=(vmem,) * 2,
        scratch_shapes=scratch,
        compiler_params=pltpu.CompilerParams(
            collective_id=0, has_side_effects=True, vmem_limit_bytes=56 * 1024 * 1024
        ),
    )(
        x,
        dim_owner.reshape(tile),
        dim_slot.reshape(tile),
        fact_owner.reshape(tile),
        fact_slot.reshape(tile),
        table,
        h,
        w_msg,
        w_self,
        w_neigh,
        cot,
    )
    return pl.pallas_call(
        hand_out,
        out_shape=(
            jax.ShapeDtypeStruct((W, W), BF),
            jax.ShapeDtypeStruct((8, W), F32),
            jax.ShapeDtypeStruct((8, W), F32),
            jax.ShapeDtypeStruct((8, W), F32),
            jax.ShapeDtypeStruct((W, W), F32),
        ),
        in_specs=[vmem] * 2,
        out_specs=(vmem,) * 5,
    )(out, sums)


def solution(mesh):
    placed = (
        P("fact", "feat"),
        P("fact", None),
        P("fact"),
        P("fact", None),
        P("fact"),
        P("fact", "feat"),
        P("fact", "feat"),
        P(None, "feat"),
        P(None, "feat"),
        P(None, "feat"),
        P("fact", "feat"),
    )
    return jax.shard_map(
        shards,
        mesh=mesh,
        in_specs=placed,
        out_specs=(P("fact", "feat"),) * 5,
        check_vma=False,
    )
```

time: 121 us -> 95.3 us (0.79)
  Pallas kernels: 116 us -> 93.6 us
  local copies, waits for them, and re-layouts: 3.98 us -> 0 us
    pallas_call x1, Pallas kernels: 116 us -> 92.1 us  [shards(): pl.pallas_call(kernel, out_shape=(jax.ShapeDtypeStruct((W, W), BF), jax.S...]
    unnamed x13 -> x0, local copies, waits for them, and re-layouts: 3.98 us -> none
    pallas_call x0 -> x1, Pallas kernels: none -> 1.56 us  [shards(): pl.pallas_call(hand_out, out_shape=(jax.ShapeDtypeStruct((W, W), BF), jax...]
where the time goes in v2:
time: 95.3 us; the launch traced here: 94.3 us
  Pallas kernels  93.6 us (98%)
    pallas_call x1, Pallas kernels, shards(): pl.pallas_call(kernel, out_shape=(jax.ShapeDtypeStruct((W, W), BF), jax.S...  92.1 us

profile of v2, /device:TPU:8, one launch (start us, length us, event | category | flops | bytes accessed | tf_op | source)
XLA Modules:
  0.0 94.3 jit_solution(8028356899831308342)
XLA Ops:
  0.6 92.1 %shard_map.146 = (bf16[128,128]{1,0:T(8,128)(2,1)}, f32[160,128]{1,0:T(8,128)}) custom-call(bf16[1024,128]{1,0:T(8,128)(2,1)} %x_ref.1, s32[8,128]{1,0:T(8,128)} %bitcast.4, s32[8,128]{1,0:T(8,128)} %bitcast.5, s32[8,128]{1,0:T(8,128)} %bitcast.6, s32[8,128]{1,0:T(8,128)} %bitcast.7, bf16[128,128]{1,0:T(8,128)(2,1)} %table_ref.1, bf16[128,128]{1,0:T(8,128)(2,1)} %h_ref.1, ...), custom_call_target="tpu_custom_call" | custom-call | tf_op jit(solution)/shard_map/pallas_call | solution.py:728
  92.7 1.6 %shard_map.147 = (bf16[128,128]{1,0:T(8,128)(2,1)}, f32[8,128]{1,0:T(8,128)}, f32[8,128]{1,0:T(8,128)}, f32[8,128]{1,0:T(8,128)}, f32[128,128]{1,0:T(8,128)}) custom-call(bf16[128,128]{1,0:T(8,128)(2,1)} %get-tuple-element.7.out_in, f32[160,128]{1,0:T(8,128)} %get-tuple-element.8.sums_in), custom_call_target="tpu_custom_call" | custom-call | tf_op jit(solution)/shard_map/pallas_call | solution.py:753

commit v3 on v2

--- a/solution.py
+++ b/solution.py
@@ -15,7 +15,7 @@
 TARGETS = (4, -3, 1, -1, 3, -2, 2, 0)
 NEAR_AT = (2, 3)
 FAR_AT = (0, 1, 4, 5, 6)
-YD = (1, 3, 2)
+YD = (2, 1, 3)
 ROWS = 1024
 TILE = 256
 W = 128
@@ -497,28 +497,23 @@
         x_landed(1)
         x_copy(5).start()
 
-    def keep(rows, found):
-        acc[rows, :] = found
-
-    gather_run(keys_dim, keep, {0: relay_x})
-
-    for n in range(2, 6):
-        x_landed(n)
-    for i in range(3):
-        h_copy(i).start()
-        c_copy(i).start()
-        w_copy(i).start()
-
-    def message_tile(t, carry):
-        rows = pl.ds(pl.multiple_of(t * TILE, TILE), TILE)
-        feats = jnp.concatenate([xs[b, rows, :] for b in range(4)], axis=1)
-        v = acc[rows, :] + jnp.dot(feats, wm[...], preferred_element_type=F32)
+    def encode():
+        for n in range(2, 6):
+            x_landed(n)
+        for i in range(3):
+            h_copy(i).start()
+            c_copy(i).start()
+            w_copy(i).start()
+        feats = jnp.concatenate([xs[b] for b in range(4)], axis=1)
+        acc[...] = jnp.dot(feats, wm[...], preferred_element_type=F32)
+
+    def message(rows, found):
+        v = acc[rows, :] + found
         s = sigmoid_of(v)
         val[rows, :] = (v * s).astype(BF)
         slope[rows, :] = s * (1.0 + v * (1.0 - s))
-        return carry
-
-    lax.fori_loop(0, ROWS // TILE, message_tile, 0)
+
+    gather_run(keys_dim, message, {0: relay_x, 17: encode})
     gather_drain()
 
     for d in range(1, 8):
@@ -545,6 +540,19 @@
         h_full = jnp.concatenate([hx[b] for b in range(4)], axis=1)
         for b in range(4):
             pre[b] = jnp.dot(h_full, w2[0, b], preferred_element_type=F32)
+
+    def divide_by():
+        for d in range(1, 8):
+            landed(cr2.at[d - 1], s_n2.at[d - 1], r_n2.at[d - 1])
+        hsum = cs[...]
+        for d in range(1, 8):
+            hsum = hsum + cr2[d - 1]
+        row_no = lax.broadcasted_iota(jnp.int32, (8, W), 0)
+        mine_row = jnp.sum(jnp.where(row_no == q, hsum, 0.0), axis=0, keepdims=True)
+        column = jnp.sum(
+            jnp.where(eye, jnp.broadcast_to(mine_row, (W, W)), 0.0), axis=1, keepdims=True
+        )
+        div[...] = jnp.broadcast_to(jnp.maximum(column, 1.0), (W, W))
 
     drain1 = reduce_all(
         val,
@@ -558,20 +566,8 @@
         zrecv1,
         res1,
         False,
-        {8: weights_on, 10: from_entities},
+        {8: weights_on, 9: divide_by, 10: from_entities},
     )
-
-    for d in range(1, 8):
-        landed(cr2.at[d - 1], s_n2.at[d - 1], r_n2.at[d - 1])
-    hsum = cs[...]
-    for d in range(1, 8):
-        hsum = hsum + cr2[d - 1]
-    row_no = lax.broadcasted_iota(jnp.int32, (8, W), 0)
-    mine_row = jnp.sum(jnp.where(row_no == q, hsum, 0.0), axis=0, keepdims=True)
-    column = jnp.sum(
-        jnp.where(eye, jnp.broadcast_to(mine_row, (W, W)), 0.0), axis=1, keepdims=True
-    )
-    div[...] = jnp.broadcast_to(jnp.maximum(column, 1.0), (W, W))
 
     ax[g] = (res1[...] / div[...]).astype(BF)
     for i in range(3):

time: 95.3 us -> 93.2 us (0.978)
  Pallas kernels: 93.6 us -> 92.3 us
    pallas_call x1, Pallas kernels: 92.1 us -> 90.8 us  [shards(): pl.pallas_call(kernel, out_shape=(jax.ShapeDtypeStruct((W, W), BF), jax.S...]
where the time goes in v3:
time: 93.2 us; the launch traced here: 93 us
  Pallas kernels  92.3 us (99%)
    pallas_call x1, Pallas kernels, shards(): pl.pallas_call(kernel, out_shape=(jax.ShapeDtypeStruct((W, W), BF), jax.S...  90.8 us

profile of v3, /device:TPU:8, one launch (start us, length us, event | category | flops | bytes accessed | tf_op | source)
XLA Modules:
  0.0 93.0 jit_solution(17815531561434212531)
XLA Ops:
  0.6 90.8 %shard_map.146 = (bf16[128,128]{1,0:T(8,128)(2,1)}, f32[160,128]{1,0:T(8,128)}) custom-call(bf16[1024,128]{1,0:T(8,128)(2,1)} %x_ref.1, s32[8,128]{1,0:T(8,128)} %bitcast.4, s32[8,128]{1,0:T(8,128)} %bitcast.5, s32[8,128]{1,0:T(8,128)} %bitcast.6, s32[8,128]{1,0:T(8,128)} %bitcast.7, bf16[128,128]{1,0:T(8,128)(2,1)} %table_ref.1, bf16[128,128]{1,0:T(8,128)(2,1)} %h_ref.1, ...), custom_call_target="tpu_custom_call" | custom-call | tf_op jit(solution)/shard_map/pallas_call | solution.py:724
  91.4 1.6 %shard_map.147 = (bf16[128,128]{1,0:T(8,128)(2,1)}, f32[8,128]{1,0:T(8,128)}, f32[8,128]{1,0:T(8,128)}, f32[8,128]{1,0:T(8,128)}, f32[128,128]{1,0:T(8,128)}) custom-call(bf16[128,128]{1,0:T(8,128)(2,1)} %get-tuple-element.7.out_in, f32[160,128]{1,0:T(8,128)} %get-tuple-element.8.sums_in), custom_call_target="tpu_custom_call" | custom-call | tf_op jit(solution)/shard_map/pallas_call | solution.py:749

commit v4 on v3

--- a/solution.py
+++ b/solution.py
@@ -21,6 +21,7 @@
 W = 128
 EXTRA = 160
 LAG = 5
+SPLIT = (0, 6, 7)
 
 
 def sigmoid_of(v):
@@ -292,7 +293,7 @@
             flipped = oint + c * (1 - 2 * lax.rem(oint, 2))
             owners_t[:, span] = jnp.broadcast_to(flipped.astype(F32), (W, W)).astype(BF)
 
-    def reduce_block(j, source, psend, grads):
+    def reduce_block(j, source, psend, grads, send):
         tz = zs[TARGETS[j] % NZ]
         owners_t, slots_t = (ot_dim, bt_dim) if grads else (ot_ent, bt_ent)
 
@@ -300,18 +301,27 @@
         rel = owners_t[...] - jnp.full((W, ROWS), base, F32).astype(BF)
         ones = slots_t[...]
         zero = jnp.zeros_like(ones)
-        lhs = jnp.concatenate(
-            [
-                jnp.where(rel == jnp.asarray(yy * 2 + side, BF), ones, zero)
-                for side in (1, 0)
-                for yy in range(NY)
-            ],
-            axis=0,
-        )
-        got = jnp.dot(lhs, source[...], preferred_element_type=F32)
+        def product(sides):
+            lhs = jnp.concatenate(
+                [
+                    jnp.where(rel == jnp.asarray(yy * 2 + side, BF), ones, zero)
+                    for side in sides
+                    for yy in range(NY)
+                ],
+                axis=0,
+            )
+            return jnp.dot(lhs, source[...], preferred_element_type=F32)
+
+        def blocks(got, first):
+            return [got[(first + yy) * W : (first + yy + 1) * W] for yy in range(NY)]
+
+        if j in SPLIT:
+            theirs = blocks(product((1,)), 0)
+        else:
+            got = product((1, 0))
+            theirs, ours = blocks(got, 0), blocks(got, NY)
         for yy in range(NY):
-            psend[j, yy, 0:W] = got[yy * W : (yy + 1) * W].astype(BF)
-            pown[j, yy, 0:W] = got[(NY + yy) * W : (NY + yy + 1) * W]
+            psend[j, yy, 0:W] = theirs[yy].astype(BF)
         if grads:
             blank = jnp.zeros((8, W), F32)
             for yy in range(NY):
@@ -327,6 +337,11 @@
                 psend[j, yy, W + 16 : W + 32] = jnp.concatenate(
                     [gw[2, other, :], blank], axis=0
                 ).astype(BF)
+        send()
+        if j in SPLIT:
+            ours = blocks(product((0,)), 0)
+        for yy in range(NY):
+            pown[j, yy, 0:W] = ours[yy]
 
     def reduce_all(
         source, psend, precv, gsend, grecv, ysend, yrecv, zsend, zrecv, res, grads, hooks
@@ -388,8 +403,7 @@
 
         for step in range(8 + LAG):
             if step < 8:
-                reduce_block(step, source, psend, grads)
-                to_mate(step).start()
+                reduce_block(step, source, psend, grads, to_mate(step).start)
             if 1 <= step < 9:
                 stage1(step - 1)
             if step in hooks:

time: 93.2 us -> 92.8 us (level)
  no operation moved by 1% of the time
where the time goes in v4:
time: 92.8 us; the launch traced here: 92.6 us
  Pallas kernels  91.9 us (99%)
    pallas_call x1, Pallas kernels, shards(): pl.pallas_call(kernel, out_shape=(jax.ShapeDtypeStruct((W, W), BF), jax.S...  90.4 us

profile of v4, /device:TPU:8, one launch (start us, length us, event | category | flops | bytes accessed | tf_op | source)
XLA Modules:
  0.0 92.6 jit_solution(4953501001557151304)
XLA Ops:
  0.6 90.4 %shard_map.146 = (bf16[128,128]{1,0:T(8,128)(2,1)}, f32[160,128]{1,0:T(8,128)}) custom-call(bf16[1024,128]{1,0:T(8,128)(2,1)} %x_ref.1, s32[8,128]{1,0:T(8,128)} %bitcast.4, s32[8,128]{1,0:T(8,128)} %bitcast.5, s32[8,128]{1,0:T(8,128)} %bitcast.6, s32[8,128]{1,0:T(8,128)} %bitcast.7, bf16[128,128]{1,0:T(8,128)(2,1)} %table_ref.1, bf16[128,128]{1,0:T(8,128)(2,1)} %h_ref.1, ...), custom_call_target="tpu_custom_call" | custom-call | tf_op jit(solution)/shard_map/pallas_call | solution.py:738
  91.0 1.6 %shard_map.147 = (bf16[128,128]{1,0:T(8,128)(2,1)}, f32[8,128]{1,0:T(8,128)}, f32[8,128]{1,0:T(8,128)}, f32[8,128]{1,0:T(8,128)}, f32[128,128]{1,0:T(8,128)}) custom-call(bf16[128,128]{1,0:T(8,128)(2,1)} %get-tuple-element.7.out_in, f32[160,128]{1,0:T(8,128)} %get-tuple-element.8.sums_in), custom_call_target="tpu_custom_call" | custom-call | tf_op jit(solution)/shard_map/pallas_call | solution.py:763

commit v5 on v4

--- a/solution.py
+++ b/solution.py
@@ -21,7 +21,7 @@
 W = 128
 EXTRA = 160
 LAG = 5
-SPLIT = (0, 6, 7)
+SPLIT = (0, 1, 5, 6, 7)
 
 
 def sigmoid_of(v):

time: 92.8 us -> 92.4 us (level)
  Pallas kernels: 91.9 us -> 90.8 us
    pallas_call x1, Pallas kernels: 90.4 us -> 89.2 us  [shards(): pl.pallas_call(kernel, out_shape=(jax.ShapeDtypeStruct((W, W), BF), jax.S...]
where the time goes in v5:
time: 92.4 us; the launch traced here: 91.4 us
  Pallas kernels  90.8 us (98%)
    pallas_call x1, Pallas kernels, shards(): pl.pallas_call(kernel, out_shape=(jax.ShapeDtypeStruct((W, W), BF), jax.S...  89.2 us

profile of v5, /device:TPU:8, one launch (start us, length us, event | category | flops | bytes accessed | tf_op | source)
XLA Modules:
  0.0 91.4 jit_solution(10984683069924650785)
XLA Ops:
  0.6 89.2 %shard_map.146 = (bf16[128,128]{1,0:T(8,128)(2,1)}, f32[160,128]{1,0:T(8,128)}) custom-call(bf16[1024,128]{1,0:T(8,128)(2,1)} %x_ref.1, s32[8,128]{1,0:T(8,128)} %bitcast.4, s32[8,128]{1,0:T(8,128)} %bitcast.5, s32[8,128]{1,0:T(8,128)} %bitcast.6, s32[8,128]{1,0:T(8,128)} %bitcast.7, bf16[128,128]{1,0:T(8,128)(2,1)} %table_ref.1, bf16[128,128]{1,0:T(8,128)(2,1)} %h_ref.1, ...), custom_call_target="tpu_custom_call" | custom-call | tf_op jit(solution)/shard_map/pallas_call | solution.py:738
  89.8 1.6 %shard_map.147 = (bf16[128,128]{1,0:T(8,128)(2,1)}, f32[8,128]{1,0:T(8,128)}, f32[8,128]{1,0:T(8,128)}, f32[8,128]{1,0:T(8,128)}, f32[128,128]{1,0:T(8,128)}) custom-call(bf16[128,128]{1,0:T(8,128)(2,1)} %get-tuple-element.7.out_in, f32[160,128]{1,0:T(8,128)} %get-tuple-element.8.sums_in), custom_call_target="tpu_custom_call" | custom-call | tf_op jit(solution)/shard_map/pallas_call | solution.py:763
